TPU v7x, 32 devices: a whole 2x2x4 slice. The times are simulated.
32 devices in a mesh: dp: 2 (over core), row: 4 (over y, x), col: 4 (over z).
Axes of the slice: x: 2, y: 2, z: 4, core: 2. Of those that a mesh axis runs over, the one named last changes fastest.
Arguments:
- tokens: bfloat16 [768, 32768], P('col', ('dp', 'row')), may hold values from -6 to 6
- w_qkv: bfloat16 [768, 3, 768], P(('dp', 'row'), None, 'col'), may hold values from -0.3125 to 0.3125
- bias_qv: float32 [2, 768], P(None, 'col'), may hold values from -3 to 3
- w_attn_out: bfloat16 [768, 768], P(('dp', 'row'), 'col'), may hold values from -0.875 to 0.875
- bias_attn_out: float32 [768], P('col'), may hold values from -3 to 3
- w_in: bfloat16 [768, 3072], P(('dp', 'row'), 'col'), may hold values from -0.21875 to 0.21875
- bias_in: float32 [3072], P('col'), may hold values from -3 to 3
- w_out: bfloat16 [768, 3072], P(('dp', 'row'), 'col'), may hold values from -0.21875 to 0.21875
- bias_out: float32 [768], P('col'), may hold values from -3 to 3
- norm_gains: float32 [2, 768], P(None, 'col'), may hold values from 0.5 to 1.5
- norm_biases: float32 [2, 768], P(None, 'col'), may hold values from -3 to 3
- seq_lengths: int32 [32], P(('dp', 'row')), may hold values from 256 to 1024, as said below
- seq_offsets: int32 [32], P(('dp', 'row')), may hold values from 0 to 768, as said below
- cotangent: bfloat16 [768, 32768], P('col', ('dp', 'row')), may hold values from -6 to 6
Outputs:
- activations: float32 [768, 32768], P('col', ('dp', 'row'))
- token_grad: float32 [768, 32768], P('col', ('dp', 'row'))
- grad_qkv: float32 [768, 3, 768], P(('dp', 'row'), None, 'col')
- grad_bias_qv: float32 [2, 768], P(None, 'col')
- grad_attn_out: float32 [768, 768], P(('dp', 'row'), 'col')
- grad_bias_attn_out: float32 [768], P('col')
- grad_in: float32 [768, 3072], P(('dp', 'row'), 'col')
- grad_bias_in: float32 [3072], P('col')
- grad_out: float32 [768, 3072], P(('dp', 'row'), 'col')
- grad_bias_out: float32 [768], P('col')
- grad_norm_gains: float32 [2, 768], P(None, 'col')
- grad_norm_biases: float32 [2, 768], P(None, 'col')
Inputs may be any that keep to these rules, and one draw needn't show every extreme that they name: seq_lengths[j] is the length of the one sequence of window j (tokens j * 1024 to (j + 1) * 1024 - 1); 1024 and 256 occur in every draw. seq_offsets[j] + seq_lengths[j] <= 1024: the sequence lies inside its window, the rest of the window is padding.
All inputs are finite; a program needn't handle non-finite values.
Results may differ from a plain program's by a relative error of at most 0.014.
The roundings to bfloat16 on the way count: a program that leaves them out, or rounds other values in their place, can miss the bound.
Values may be sent and summed in bfloat16 or wider, within the bound.
A program may use at most 192 MiB of HBM per device.

v0:
```python
import jax
import jax.numpy as jnp
from jax import lax
from jax.sharding import PartitionSpec as P

D = 768
HEAD_DIM = 64
PACK = 2048
SEQ_MAX = 1024
QBLOCK = 512
EPSILON = 1e-12


def row_totals(first, second):
    return lax.psum((jnp.sum(first, axis=1), jnp.sum(second, axis=1)), "col")


def norm_forward(values, gain_row, shift_row):
    totals = row_totals(values, values * values)
    average = totals[0] / D
    spread = totals[1] / D - average * average
    inverse = lax.rsqrt(spread + EPSILON)
    scaled = (values - average[:, None]) * inverse[:, None]
    return (scaled * gain_row + shift_row, scaled, inverse)


def norm_backward(upstream, scaled, inverse, gain_row):
    weighted = upstream * gain_row
    totals = row_totals(weighted, weighted * scaled)
    return inverse[:, None] * (
        weighted - (totals[0] / D)[:, None] - scaled * (totals[1] / D)[:, None]
    )


def input_total(partial_rows):
    return lax.psum_scatter(partial_rows, "col", scatter_dimension=1, tiled=True)


def grad_rows(values):
    return lax.all_gather(values, "col", axis=1, tiled=True)


def masked_scores(query_block, key_rows, live_mask, first_row):
    scores = jnp.einsum(
        "wqhe,wkhe->whqk", query_block, key_rows, preferred_element_type=jnp.float32
    ) * HEAD_DIM ** (-0.5)
    allowed = live_mask[:, first_row : first_row + QBLOCK, None] == live_mask[:, None, :]
    return jnp.where(allowed[:, None], scores, -1e30)


def attend_forward(queries, key_rows, values, live_mask):
    outputs = []
    log_totals = []
    for first_row in range(0, SEQ_MAX, QBLOCK):
        scores = masked_scores(
            queries[:, first_row : first_row + QBLOCK], key_rows, live_mask, first_row
        )
        largest = jnp.max(scores, axis=-1, keepdims=True)
        exponent = jnp.exp(scores - largest)
        row_total = jnp.sum(exponent, axis=-1, keepdims=True)
        soft_weights = (exponent / row_total).astype(jnp.bfloat16)
        outputs.append(
            jnp.einsum("whqk,wkhe->wqhe", soft_weights, values, preferred_element_type=jnp.float32)
        )
        log_totals.append(largest + jnp.log(row_total))
    return (jnp.concatenate(outputs, axis=1), log_totals)


def attend_backward(queries, key_rows, values, live_mask, log_totals, d_attended):
    score_scale = HEAD_DIM ** (-0.5)
    grad_keys = jnp.zeros(key_rows.shape, jnp.float32)
    grad_values = jnp.zeros(values.shape, jnp.float32)
    grad_queries = []
    for block_index in range(SEQ_MAX // QBLOCK):
        first_row = block_index * QBLOCK
        query_block = queries[:, first_row : first_row + QBLOCK]
        grad_block = d_attended[:, first_row : first_row + QBLOCK]
        scores = masked_scores(query_block, key_rows, live_mask, first_row)
        soft_weights = jnp.exp(scores - log_totals[block_index])
        d_weights = jnp.einsum(
            "wqhe,wkhe->whqk", grad_block, values, preferred_element_type=jnp.float32
        )
        centre = jnp.sum(soft_weights * d_weights, axis=-1, keepdims=True)
        d_scores = (soft_weights * (d_weights - centre)).astype(jnp.bfloat16)
        grad_queries.append(
            jnp.einsum("whqk,wkhe->wqhe", d_scores, key_rows, preferred_element_type=jnp.float32)
            * score_scale
        )
        grad_keys = (
            grad_keys
            + jnp.einsum(
                "whqk,wqhe->wkhe", d_scores, query_block, preferred_element_type=jnp.float32
            )
            * score_scale
        )
        grad_values = grad_values + jnp.einsum(
            "whqk,wqhe->wkhe",
            soft_weights.astype(jnp.bfloat16),
            grad_block,
            preferred_element_type=jnp.float32,
        )
    return (jnp.concatenate(grad_queries, axis=1), grad_keys, grad_values)


def contract_last(left, right):
    return lax.dot_general(
        left, right, (((1,), (1,)), ((), ())), preferred_element_type=jnp.float32
    )


def contract_first(left, right):
    return lax.dot_general(
        left, right, (((0,), (0,)), ((), ())), preferred_element_type=jnp.float32
    )


def local(
    tokens,
    w_qkv,
    bias_qv,
    w_attn_out,
    bias_attn_out,
    w_in,
    bias_in,
    w_out,
    bias_out,
    norm_gains,
    norm_biases,
    seq_lengths,
    seq_offsets,
    cotangent,
):
    part_width = tokens.shape[0]
    head_width = w_qkv.shape[2]
    head_count = head_width // HEAD_DIM
    micro_count = tokens.shape[1] // PACK
    windows = PACK // SEQ_MAX
    window_shape = (windows, SEQ_MAX, head_count, HEAD_DIM)
    places = jnp.arange(SEQ_MAX, dtype=jnp.int32)
    weight_zero = (
        jnp.zeros(w_qkv.shape, jnp.float32),
        jnp.zeros(w_attn_out.shape, jnp.float32),
        jnp.zeros(w_in.shape, jnp.float32),
        jnp.zeros(w_out.shape, jnp.float32),
    )
    small_zero = (
        jnp.zeros(bias_qv.shape, jnp.float32),
        jnp.zeros(bias_attn_out.shape, jnp.float32),
        jnp.zeros(bias_in.shape, jnp.float32),
        jnp.zeros(bias_out.shape, jnp.float32),
        jnp.zeros(norm_gains.shape, jnp.float32),
        jnp.zeros(norm_biases.shape, jnp.float32),
    )

    def micro_step(carried, inputs):
        token_cols, upstream_cols, lengths, offsets = inputs
        weight_sums, small_sums = carried
        gathered = (
            lax.all_gather(w_qkv, ("dp", "row"), axis=0, tiled=True),
            lax.all_gather(w_attn_out, ("dp", "row"), axis=0, tiled=True),
            lax.all_gather(w_in, ("dp", "row"), axis=0, tiled=True),
            lax.all_gather(w_out, ("dp", "row"), axis=0, tiled=True),
        )
        full_qkv, full_attn_out, full_in, full_out = gathered
        live_mask = (places[None, :] >= offsets[:, None]) & (
            places[None, :] < offsets[:, None] + lengths[:, None]
        )
        live_rows = live_mask.reshape(PACK).astype(jnp.float32)[:, None]
        token_full_cols = lax.all_gather(token_cols, "col", axis=0, tiled=True)
        projected = jnp.einsum(
            "dt,dke->tke", token_full_cols, full_qkv, preferred_element_type=jnp.float32
        )
        queries = (projected[:, 0] + bias_qv[0]).astype(jnp.bfloat16).reshape(window_shape)
        key_rows = projected[:, 1].astype(jnp.bfloat16).reshape(window_shape)
        values = (projected[:, 2] + bias_qv[1]).astype(jnp.bfloat16).reshape(window_shape)
        attended, log_totals = attend_forward(queries, key_rows, values, live_mask)
        attended = attended.reshape(PACK, head_width).astype(jnp.bfloat16)
        branch = lax.psum_scatter(
            contract_last(attended, full_attn_out), "col", scatter_dimension=1, tiled=True
        )
        first_sum = token_cols.astype(jnp.float32).T + branch + bias_attn_out
        normed, scaled_one, inverse_one = norm_forward(first_sum, norm_gains[0], norm_biases[0])
        normed_full = lax.all_gather(normed.astype(jnp.bfloat16), "col", axis=1, tiled=True)
        hidden = jnp.dot(normed_full, full_in, preferred_element_type=jnp.float32) + bias_in
        active_low = jax.nn.gelu(hidden, approximate=False).astype(jnp.bfloat16)
        second = lax.psum_scatter(
            contract_last(active_low, full_out), "col", scatter_dimension=1, tiled=True
        )
        second_sum = normed + second + bias_out
        result, scaled_two, inverse_two = norm_forward(second_sum, norm_gains[1], norm_biases[1])
        activations = (result * live_rows).T
        regathered = (
            lax.all_gather(w_qkv, ("dp", "row"), axis=0, tiled=True),
            lax.all_gather(w_attn_out, ("dp", "row"), axis=0, tiled=True),
            lax.all_gather(w_in, ("dp", "row"), axis=0, tiled=True),
            lax.all_gather(w_out, ("dp", "row"), axis=0, tiled=True),
        )
        back_qkv, back_attn_out, back_in, back_out = regathered
        upstream = upstream_cols.astype(jnp.float32).T * live_rows
        gain_two = jnp.sum(upstream * scaled_two, axis=0)
        shift_two = jnp.sum(upstream, axis=0)
        d_second = norm_backward(upstream, scaled_two, inverse_two, norm_gains[1])
        bias_out_grad = jnp.sum(d_second, axis=0)
        d_second_full = grad_rows(d_second.astype(jnp.bfloat16))
        out_grad = contract_first(d_second_full, active_low)
        d_active = jnp.dot(d_second_full, back_out, preferred_element_type=jnp.float32)
        gelu_pull = jax.vjp(lambda pre_act: jax.nn.gelu(pre_act, approximate=False), hidden)[1]
        d_hidden = gelu_pull(d_active)[0]
        bias_in_grad = jnp.sum(d_hidden, axis=0)
        d_hidden_low = d_hidden.astype(jnp.bfloat16)
        in_grad = contract_first(normed_full, d_hidden_low)
        d_normed = d_second + input_total(contract_last(d_hidden_low, back_in))
        gain_one = jnp.sum(d_normed * scaled_one, axis=0)
        shift_one = jnp.sum(d_normed, axis=0)
        d_first = norm_backward(d_normed, scaled_one, inverse_one, norm_gains[0])
        bias_attn_grad = jnp.sum(d_first, axis=0)
        d_first_full = grad_rows(d_first.astype(jnp.bfloat16))
        attn_out_grad = contract_first(d_first_full, attended)
        d_attended = jnp.dot(
            d_first_full, back_attn_out, preferred_element_type=jnp.float32
        ).astype(jnp.bfloat16)
        grad_q, grad_k, grad_v = attend_backward(
            queries, key_rows, values, live_mask, log_totals, d_attended.reshape(window_shape)
        )
        grad_q = grad_q.reshape(PACK, head_width)
        grad_k = grad_k.reshape(PACK, head_width)
        grad_v = grad_v.reshape(PACK, head_width)
        qv_grad = jnp.stack([jnp.sum(grad_q, axis=0), jnp.sum(grad_v, axis=0)])
        d_projected = jnp.stack([grad_q, grad_k, grad_v], axis=1).astype(jnp.bfloat16)
        qkv_grad = jnp.einsum(
            "dt,tke->dke", token_full_cols, d_projected, preferred_element_type=jnp.float32
        )
        token_grad = (
            d_first
            + input_total(
                jnp.einsum("tke,dke->td", d_projected, back_qkv, preferred_element_type=jnp.float32)
            )
        ).T
        summed = (
            lax.psum_scatter(qkv_grad, ("dp", "row"), scatter_dimension=0, tiled=True),
            lax.psum_scatter(attn_out_grad, ("dp", "row"), scatter_dimension=0, tiled=True),
            lax.psum_scatter(in_grad, ("dp", "row"), scatter_dimension=0, tiled=True),
            lax.psum_scatter(out_grad, ("dp", "row"), scatter_dimension=0, tiled=True),
        )
        weight_sums = jax.tree.map(jnp.add, weight_sums, summed)
        small_terms = (
            qv_grad,
            bias_attn_grad,
            bias_in_grad,
            bias_out_grad,
            jnp.stack([gain_one, gain_two]),
            jnp.stack([shift_one, shift_two]),
        )
        small_sums = jax.tree.map(jnp.add, small_sums, small_terms)
        return ((weight_sums, small_sums), (activations, token_grad))

    token_blocks = tokens.reshape(part_width, micro_count, PACK).transpose(1, 0, 2)
    upstream_blocks = cotangent.reshape(part_width, micro_count, PACK).transpose(1, 0, 2)
    inputs = (
        token_blocks,
        upstream_blocks,
        seq_lengths.reshape(micro_count, windows),
        seq_offsets.reshape(micro_count, windows),
    )
    finals, stacked = lax.scan(micro_step, (weight_zero, small_zero), inputs)
    weight_sums, small_sums = finals
    small_sums = lax.psum(
        (small_sums[0], small_sums[1], small_sums[2], small_sums[3], small_sums[4], small_sums[5]),
        ("dp", "row"),
    )
    activations = stacked[0].transpose(1, 0, 2).reshape(part_width, micro_count * PACK)
    token_grads = stacked[1].transpose(1, 0, 2).reshape(part_width, micro_count * PACK)
    return (
        activations,
        token_grads,
        weight_sums[0],
        small_sums[0],
        weight_sums[1],
        small_sums[1],
        weight_sums[2],
        small_sums[2],
        weight_sums[3],
        small_sums[3],
        small_sums[4],
        small_sums[5],
    )


def solution(mesh):
    return jax.shard_map(
        local,
        mesh=mesh,
        in_specs=(
            P("col", ("dp", "row")),
            P(("dp", "row"), None, "col"),
            P(None, "col"),
            P(("dp", "row"), "col"),
            P("col"),
            P(("dp", "row"), "col"),
            P("col"),
            P(("dp", "row"), "col"),
            P("col"),
            P(None, "col"),
            P(None, "col"),
            P(("dp", "row")),
            P(("dp", "row")),
            P("col", ("dp", "row")),
        ),
        out_specs=(
            P("col", ("dp", "row")),
            P("col", ("dp", "row")),
            P(("dp", "row"), None, "col"),
            P(None, "col"),
            P(("dp", "row"), "col"),
            P("col"),
            P(("dp", "row"), "col"),
            P("col"),
            P(("dp", "row"), "col"),
            P("col"),
            P(None, "col"),
            P(None, "col"),
        ),
        check_vma=False,
    )
```

profile of v0, /device:TPU:1, one launch (start us, length us, event | category | flops | bytes accessed | tf_op | source)
XLA Modules:
  0.0 2196.4 jit_solution(1545050451613228207)
XLA Ops:
  19.6 2135.8 %while.34 = (s32[]{:T(128)}, f32[96,3,192]{2,0,1:T(8,128)}, f32[96,192]{1,0:T(8,128)}, f32[96,768]{1,0:T(8,128)}, f32[96,768]{1,0:T(8,128)}, /*index=5*/f32[2,19...) while((s32[]{:T(128)}, f32[96,3,192]{2,0,1:T(8,128)}, ...), condition=%wide.region_41.42_spmd.clone.clone, body=%wide.region_0.41_spmd.clone.clone.sunk | while | flops 26853322752 | bytes 1020480256 | solution.py:265
  21.6 35.5 %all_gather.50 = bf16[768,3,192]{2,1,0:T(4,128)(2,1)S(1)} all-gather(bf16[96,3,192]{2,1,0:T(4,128)(2,1)} %get-tuple-element.915), channel_id=1, replica_groups=mesh['dp'=2,'row'=4,'col'=4] {'dp','row'}, dimensions={0}, use_global_device_ids=true | all-gather | bytes 995328 | tf_op jit(solution)/shard_map/while/body/eval_jaxpr/all_gather | solution.py:159
  59.3 24.1 %all_gather.51 = bf16[768,192]{1,0:T(8,128)(2,1)S(1)} all-gather(bf16[96,192]{1,0:T(8,128)(2,1)S(1)} %copy-done.45), channel_id=1, replica_groups=mesh['dp'=2,'row'=4,'col'=4] {'dp','row'}, dimensions={0}, use_global_device_ids=true | all-gather | bytes 331776 | tf_op jit(solution)/shard_map/while/body/eval_jaxpr/all_gather | solution.py:160
  130.9 106.3 %reduce-scatter.9.cloned.1.call-done = f32[2048,192]{0,1:T(8,128)} async-done(((f32[2048,768]{0,1:T(8,128)}), f32[2048,192]{0,1:T(8,128)}) %reduce-scatter.9.cloned.1.call-update) | async-done | bytes 1572880 | tf_op jit(solution)/shard_map/while/body/eval_jaxpr/reduce_scatter | solution.py:178
  263.9 64.9 %all-gather.13.cloned.1.call-done = bf16[2048,768]{0,1:T(8,128)(2,1)} async-done(((bf16[2048,192]{0,1:T(8,128)(2,1)}), bf16[2048,768]{0,1:T(8,128)(2,1)}) %all-gather.13.cloned.1.call-update) | async-done | bytes 3145744 | tf_op jit(solution)/shard_map/while/body/eval_jaxpr/all_gather | solution.py:183
  361.9 109.8 %reduce-scatter.11.cloned.1.call-done = f32[2048,192]{0,1:T(8,128)} async-done(((f32[2048,768]{0,1:T(8,128)}), f32[2048,192]{0,1:T(8,128)}) %reduce-scatter.11.cloned.1.call-update) | async-done | bytes 1572880 | tf_op jit(solution)/shard_map/while/body/eval_jaxpr/reduce_scatter | solution.py:186
  511.5 69.3 %all-gather.19.cloned.1.call-done = bf16[2048,768]{0,1:T(8,128)(2,1)} async-done(((bf16[2048,192]{0,1:T(8,128)(2,1)}), bf16[2048,768]{0,1:T(8,128)(2,1)}) %all-gather.19.cloned.1.call-update) | async-done | bytes 3145744 | tf_op jit(solution)/shard_map/while/body/eval_jaxpr/all_gather | solution.py:40
  598.3 109.6 %reduce-scatter.13.cloned.1.call-done = f32[2048,192]{0,1:T(8,128)} async-done(((f32[2048,768]{0,1:T(8,128)}), f32[2048,192]{0,1:T(8,128)}) %reduce-scatter.13.cloned.1.call-update) | async-done | bytes 1572880 | tf_op jit(solution)/shard_map/while/body/eval_jaxpr/reduce_scatter | solution.py:36
  747.3 50.7 %all-gather.21.cloned.1.call-done = bf16[2048,768]{0,1:T(8,128)(2,1)} async-done(((bf16[2048,192]{0,1:T(8,128)(2,1)}), bf16[2048,768]{0,1:T(8,128)(2,1)}) %all-gather.21.cloned.1.call-update) | async-done | bytes 3145744 | tf_op jit(solution)/shard_map/while/body/eval_jaxpr/all_gather | solution.py:40
  898.4 27.1 %reduce-scatter.17.cloned.1.call-done = f32[96,192]{1,0:T(8,128)} async-done(((f32[768,192]{1,0:T(8,128)}), f32[96,192]{1,0:T(8,128)}) %reduce-scatter.17.cloned.1.call-update) | async-done | bytes 73744 | tf_op jit(solution)/shard_map/while/body/eval_jaxpr/reduce_scatter | solution.py:241
  926.4 45.2 %reduce-scatter.15.cloned.1.call-done = f32[96,3,192]{2,0,1:T(8,128)} async-done(((f32[768,3,192]{2,0,1:T(8,128)}), f32[96,3,192]{2,0,1:T(8,128)}) %reduce-scatter.15.cloned.1.call-update) | async-done | bytes 221200 | tf_op jit(solution)/shard_map/while/body/eval_jaxpr/reduce_scatter | solution.py:240
  973.3 111.4 %reduce-scatter.23.cloned.1.call-done = f32[2048,192]{0,1:T(8,128)} async-done(((f32[2048,768]{0,1:T(8,128)}), f32[2048,192]{0,1:T(8,128)}) %reduce-scatter.23.cloned.1.call-update) | async-done | bytes 1572880 | tf_op jit(solution)/shard_map/while/body/eval_jaxpr/reduce_scatter | solution.py:36
  1089.9 34.6 %all_gather.50 = bf16[768,3,192]{2,1,0:T(4,128)(2,1)S(1)} all-gather(bf16[96,3,192]{2,1,0:T(4,128)(2,1)} %get-tuple-element.915), channel_id=1, replica_groups=mesh['dp'=2,'row'=4,'col'=4] {'dp','row'}, dimensions={0}, use_global_device_ids=true | all-gather | bytes 995328 | tf_op jit(solution)/shard_map/while/body/eval_jaxpr/all_gather | solution.py:159
  1126.6 24.2 %all_gather.51 = bf16[768,192]{1,0:T(8,128)(2,1)S(1)} all-gather(bf16[96,192]{1,0:T(8,128)(2,1)S(1)} %copy-done.45), channel_id=1, replica_groups=mesh['dp'=2,'row'=4,'col'=4] {'dp','row'}, dimensions={0}, use_global_device_ids=true | all-gather | bytes 331776 | tf_op jit(solution)/shard_map/while/body/eval_jaxpr/all_gather | solution.py:160
  1196.8 106.4 %reduce-scatter.9.cloned.1.call-done = f32[2048,192]{0,1:T(8,128)} async-done(((f32[2048,768]{0,1:T(8,128)}), f32[2048,192]{0,1:T(8,128)}) %reduce-scatter.9.cloned.1.call-update) | async-done | bytes 1572880 | tf_op jit(solution)/shard_map/while/body/eval_jaxpr/reduce_scatter | solution.py:178
  1329.8 64.9 %all-gather.13.cloned.1.call-done = bf16[2048,768]{0,1:T(8,128)(2,1)} async-done(((bf16[2048,192]{0,1:T(8,128)(2,1)}), bf16[2048,768]{0,1:T(8,128)(2,1)}) %all-gather.13.cloned.1.call-update) | async-done | bytes 3145744 | tf_op jit(solution)/shard_map/while/body/eval_jaxpr/all_gather | solution.py:183
  1427.9 109.8 %reduce-scatter.11.cloned.1.call-done = f32[2048,192]{0,1:T(8,128)} async-done(((f32[2048,768]{0,1:T(8,128)}), f32[2048,192]{0,1:T(8,128)}) %reduce-scatter.11.cloned.1.call-update) | async-done | bytes 1572880 | tf_op jit(solution)/shard_map/while/body/eval_jaxpr/reduce_scatter | solution.py:186
  1577.8 69.3 %all-gather.19.cloned.1.call-done = bf16[2048,768]{0,1:T(8,128)(2,1)} async-done(((bf16[2048,192]{0,1:T(8,128)(2,1)}), bf16[2048,768]{0,1:T(8,128)(2,1)}) %all-gather.19.cloned.1.call-update) | async-done | bytes 3145744 | tf_op jit(solution)/shard_map/while/body/eval_jaxpr/all_gather | solution.py:40
  1664.6 109.6 %reduce-scatter.13.cloned.1.call-done = f32[2048,192]{0,1:T(8,128)} async-done(((f32[2048,768]{0,1:T(8,128)}), f32[2048,192]{0,1:T(8,128)}) %reduce-scatter.13.cloned.1.call-update) | async-done | bytes 1572880 | tf_op jit(solution)/shard_map/while/body/eval_jaxpr/reduce_scatter | solution.py:36
  1813.3 51.0 %all-gather.21.cloned.1.call-done = bf16[2048,768]{0,1:T(8,128)(2,1)} async-done(((bf16[2048,192]{0,1:T(8,128)(2,1)}), bf16[2048,768]{0,1:T(8,128)(2,1)}) %all-gather.21.cloned.1.call-update) | async-done | bytes 3145744 | tf_op jit(solution)/shard_map/while/body/eval_jaxpr/all_gather | solution.py:40
  1965.9 25.9 %reduce-scatter.17.cloned.1.call-done = f32[96,192]{1,0:T(8,128)} async-done(((f32[768,192]{1,0:T(8,128)}), f32[96,192]{1,0:T(8,128)}) %reduce-scatter.17.cloned.1.call-update) | async-done | bytes 73744 | tf_op jit(solution)/shard_map/while/body/eval_jaxpr/reduce_scatter | solution.py:241
  1992.8 45.0 %reduce-scatter.15.cloned.1.call-done = f32[96,3,192]{2,0,1:T(8,128)} async-done(((f32[768,3,192]{2,0,1:T(8,128)}), f32[96,3,192]{2,0,1:T(8,128)}) %reduce-scatter.15.cloned.1.call-update) | async-done | bytes 221200 | tf_op jit(solution)/shard_map/while/body/eval_jaxpr/reduce_scatter | solution.py:240
  2039.6 111.4 %reduce-scatter.23.cloned.1.call-done = f32[2048,192]{0,1:T(8,128)} async-done(((f32[2048,768]{0,1:T(8,128)}), f32[2048,192]{0,1:T(8,128)}) %reduce-scatter.23.cloned.1.call-update) | async-done | bytes 1572880 | tf_op jit(solution)/shard_map/while/body/eval_jaxpr/reduce_scatter | solution.py:36
  2159.5 27.9 %all-reduce.4 = (f32[2,192]{1,0:T(2,128)}, f32[192]{0:T(256)}, f32[768]{0:T(1024)}, f32[192]{0:T(256)}, f32[2,192]{1,0:T(2,128)}, /*index=5*/f32[2,192]{1,0:T(2,128)}) all-reduce(f32[2,192]{1,0:T(2,128)S(1)} %copy-done.54, f32[192]{0:T(256)S(1)} %copy-done.56, ...), channel_id=1, replica_groups=mesh['dp'=2,'row'=4,'col'=4] {'dp','row'}, use_global_device_ids=true, to_apply=%region_42.43 | all-reduce | flops 2304 | bytes 18432 | tf_op jit(solution)/shard_map/psum | solution.py:267
  (547 shorter events, 644.2 us)
Async XLA Ops:
  20.7 216.5 %reduce-scatter.9.cloned.1.call-start = ((), (), s32[]{:S(2)}) async-start(), calls=%async_computation.9 | async-start | bytes 7864320 | tf_op jit(solution)/shard_map/while/body/eval_jaxpr/reduce_scatter | solution.py:178
  127.4 136.5 %all-gather.15.cloned.1.call-start = ((), (), s32[]{:S(2)}) async-start(), calls=%async_computation.11 | async-start | bytes 1327104 | tf_op jit(solution)/shard_map/while/body/eval_jaxpr/all_gather | solution.py:161
  128.2 200.6 %all-gather.13.cloned.1.call-start = ((), (), s32[]{:S(2)}) async-start(), calls=%async_computation.10 | async-start | bytes 3932160 | tf_op jit(solution)/shard_map/while/body/eval_jaxpr/all_gather | solution.py:183
  255.9 215.8 %reduce-scatter.11.cloned.1.call-start = ((), (), s32[]{:S(2)}) async-start(), calls=%async_computation.13 | async-start | bytes 7864320 | tf_op jit(solution)/shard_map/while/body/eval_jaxpr/reduce_scatter | solution.py:186
  361.2 219.5 %all-gather.19.cloned.1.call-start = ((), (), s32[]{:S(2)}) async-start(), calls=%async_computation.14 | async-start | bytes 3932160 | tf_op jit(solution)/shard_map/while/body/eval_jaxpr/all_gather | solution.py:40
  511.4 196.5 %reduce-scatter.13.cloned.1.call-start = ((), (), s32[]{:S(2)}) async-start(), calls=%async_computation.15 | async-start | bytes 7864320 | tf_op jit(solution)/shard_map/while/body/eval_jaxpr/reduce_scatter | solution.py:36
  598.3 199.7 %all-gather.21.cloned.1.call-start = ((), (), s32[]{:S(2)}) async-start(), calls=%async_computation.16 | async-start | bytes 3932160 | tf_op jit(solution)/shard_map/while/body/eval_jaxpr/all_gather | solution.py:40
  732.6 156.9 %reduce-scatter.19.cloned.1.call-start = ((), (), s32[]{:S(2)}) async-start(), calls=%async_computation.19 | async-start | bytes 2654208 | tf_op jit(solution)/shard_map/while/body/eval_jaxpr/reduce_scatter | solution.py:242
  739.5 151.7 %reduce-scatter.21.cloned.1.call-start = ((), (), s32[]{:S(2)}) async-start(), calls=%async_computation.20 | async-start | bytes 2654208 | tf_op jit(solution)/shard_map/while/body/eval_jaxpr/reduce_scatter | solution.py:243
  746.8 178.7 %reduce-scatter.17.cloned.1.call-start = ((), (), s32[]{:S(2)}) async-start(), calls=%async_computation.18 | async-start | bytes 884736 | tf_op jit(solution)/shard_map/while/body/eval_jaxpr/reduce_scatter | solution.py:241
  870.9 100.7 %reduce-scatter.15.cloned.1.call-start = ((), (), s32[]{:S(2)}) async-start(), calls=%async_computation.17 | async-start | bytes 2654208 | tf_op jit(solution)/shard_map/while/body/eval_jaxpr/reduce_scatter | solution.py:240
  879.6 205.0 %reduce-scatter.23.cloned.1.call-start = ((), (), s32[]{:S(2)}) async-start(), calls=%async_computation.21 | async-start | bytes 7864320 | tf_op jit(solution)/shard_map/while/body/eval_jaxpr/reduce_scatter | solution.py:36
  1088.9 214.3 %reduce-scatter.9.cloned.1.call-start = ((), (), s32[]{:S(2)}) async-start(), calls=%async_computation.9 | async-start | bytes 7864320 | tf_op jit(solution)/shard_map/while/body/eval_jaxpr/reduce_scatter | solution.py:178
  1193.5 136.3 %all-gather.15.cloned.1.call-start = ((), (), s32[]{:S(2)}) async-start(), calls=%async_computation.11 | async-start | bytes 1327104 | tf_op jit(solution)/shard_map/while/body/eval_jaxpr/all_gather | solution.py:161
  1194.1 200.6 %all-gather.13.cloned.1.call-start = ((), (), s32[]{:S(2)}) async-start(), calls=%async_computation.10 | async-start | bytes 3932160 | tf_op jit(solution)/shard_map/while/body/eval_jaxpr/all_gather | solution.py:183
  1322.1 215.6 %reduce-scatter.11.cloned.1.call-start = ((), (), s32[]{:S(2)}) async-start(), calls=%async_computation.13 | async-start | bytes 7864320 | tf_op jit(solution)/shard_map/while/body/eval_jaxpr/reduce_scatter | solution.py:186
  1427.3 219.8 %all-gather.19.cloned.1.call-start = ((), (), s32[]{:S(2)}) async-start(), calls=%async_computation.14 | async-start | bytes 3932160 | tf_op jit(solution)/shard_map/while/body/eval_jaxpr/all_gather | solution.py:40
  1577.7 196.5 %reduce-scatter.13.cloned.1.call-start = ((), (), s32[]{:S(2)}) async-start(), calls=%async_computation.15 | async-start | bytes 7864320 | tf_op jit(solution)/shard_map/while/body/eval_jaxpr/reduce_scatter | solution.py:36
  1664.5 199.7 %all-gather.21.cloned.1.call-start = ((), (), s32[]{:S(2)}) async-start(), calls=%async_computation.16 | async-start | bytes 3932160 | tf_op jit(solution)/shard_map/while/body/eval_jaxpr/all_gather | solution.py:40
  1798.9 157.2 %reduce-scatter.19.cloned.1.call-start = ((), (), s32[]{:S(2)}) async-start(), calls=%async_computation.19 | async-start | bytes 2654208 | tf_op jit(solution)/shard_map/while/body/eval_jaxpr/reduce_scatter | solution.py:242
  1805.8 152.1 %reduce-scatter.21.cloned.1.call-start = ((), (), s32[]{:S(2)}) async-start(), calls=%async_computation.20 | async-start | bytes 2654208 | tf_op jit(solution)/shard_map/while/body/eval_jaxpr/reduce_scatter | solution.py:243
  1813.1 178.8 %reduce-scatter.17.cloned.1.call-start = ((), (), s32[]{:S(2)}) async-start(), calls=%async_computation.18 | async-start | bytes 884736 | tf_op jit(solution)/shard_map/while/body/eval_jaxpr/reduce_scatter | solution.py:241
  1937.2 100.6 %reduce-scatter.15.cloned.1.call-start = ((), (), s32[]{:S(2)}) async-start(), calls=%async_computation.17 | async-start | bytes 2654208 | tf_op jit(solution)/shard_map/while/body/eval_jaxpr/reduce_scatter | solution.py:240
  1946.0 205.1 %reduce-scatter.23.cloned.1.call-start = ((), (), s32[]{:S(2)}) async-start(), calls=%async_computation.21 | async-start | bytes 7864320 | tf_op jit(solution)/shard_map/while/body/eval_jaxpr/reduce_scatter | solution.py:36
  (133 other events, 4187.8 us)
Sparse Core Ops, SparseCore 0:
  22.5 65.3 all-gather.10
  127.6 109.5 reduce-scatter.8
  265.9 62.8 all-gather.12
  361.3 110.3 reduce-scatter.10
  511.5 69.1 all-gather.18
  598.4 109.5 reduce-scatter.12
  732.7 65.2 all-gather.20
  801.1 40.9 reduce-scatter.18
  845.5 42.3 reduce-scatter.20
  890.9 34.5 reduce-scatter.16
  928.8 42.7 reduce-scatter.14
  973.8 110.8 reduce-scatter.22
  1090.5 63.8 all-gather.10
  1193.6 109.5 reduce-scatter.8
  1331.8 62.8 all-gather.12
  1427.4 110.3 reduce-scatter.10
  1577.8 69.1 all-gather.18
  1664.7 109.5 reduce-scatter.12
  1799.0 65.2 all-gather.20
  1867.4 40.9 reduce-scatter.18
  1911.8 42.3 reduce-scatter.20
  1957.2 34.5 reduce-scatter.16
  1995.1 42.7 reduce-scatter.14
  2040.1 110.8 reduce-scatter.22
  (4 shorter events, 95.7 us)
where the time goes:
time: 2200 us
  waiting for transfers between devices  1420 us (65%)
  matrix products  266 us (12%)
  blocking collectives  264 us (12%)
  other arithmetic  136 us (6%)
  local copies, waits for them, and re-layouts  90.9 us (4%)
    reduce_scatter x4, waiting for transfers between devices, input_total(): lax.psum_scatter(partial_rows, 'col', scatter_dimension=1, tiled=True)  442 us
    all_gather x4, waiting for transfers between devices, grad_rows(): return lax.all_gather(values, 'col', axis=1, tiled=True)  240 us
    reduce_scatter x2, waiting for transfers between devices, micro_step(): lax.psum_scatter(contract_last(active_low, full_out), 'col', scatter_dime...  220 us
    reduce_scatter x2, waiting for transfers between devices, micro_step(): lax.psum_scatter(contract_last(attended, full_attn_out), 'col', scatter_d...  213 us
    all_gather x2, waiting for transfers between devices, micro_step(): lax.all_gather(normed.astype(jnp.bfloat16), 'col', axis=1, tiled=True)  130 us
    psum x8, blocking collectives, row_totals(): return lax.psum((jnp.sum(first, axis=1), jnp.sum(second, axis=1)), 'col')  117 us
    reduce_scatter x2, waiting for transfers between devices, micro_step(): lax.psum_scatter(qkv_grad, ('dp', 'row'), scatter_dimension=0, tiled=True)  90.2 us
    all_gather x2, blocking collectives, micro_step(): lax.all_gather(w_qkv, ('dp', 'row'), axis=0, tiled=True)  70.2 us
  transfers between devices with their start and end apart: 28, of which 24 were waited for; matrix products, arithmetic and copies ran while one was open for 13% of the time, Pallas kernels for 0%

commit v1 on v0

--- a/solution.py
+++ b/solution.py
@@ -2,6 +2,7 @@
 import jax.numpy as jnp
 from jax import lax
 from jax.sharding import PartitionSpec as P
+from jax.lax import axis_index, axis_size, ppermute
 
 D = 768
 HEAD_DIM = 64
@@ -37,7 +38,31 @@
 
 
 def grad_rows(values):
-    return lax.all_gather(values, "col", axis=1, tiled=True)
+
+    def move_flows_on_mesh(base_x):
+        shard_axis = "col"
+        everything, val, found_now = (
+            axis_size(shard_axis),
+            axis_index(shard_axis),
+            base_x.shape[1],
+        )
+        z2, met_up = (base_x, 1)
+        while met_up < everything:
+            z2 = jnp.concatenate(
+                [
+                    z2,
+                    ppermute(
+                        z2,
+                        shard_axis,
+                        perm=[(num, (num - met_up) % everything) for num in range(everything)],
+                    ),
+                ],
+                1,
+            )
+            met_up = 2 * met_up
+        return jnp.roll(z2, val * found_now, 1)
+
+    return move_flows_on_mesh(values)
 
 
 def masked_scores(query_block, key_rows, live_mask, first_row):

time: 2200 us -> 2270 us (1.032)
  other arithmetic: 136 us -> 177 us
  waiting for transfers between devices: 1420 us -> 1460 us
    ppermute x0 -> x8, waiting for transfers between devices: none -> 317 us  [move_flows_on_mesh(): ppermute(z2, shard_axis, perm=[(num, (num - met_up) % everything) for num...]
    all_gather x4 -> x0, waiting for transfers between devices: 240 us -> none  [grad_rows(): return lax.all_gather(values, 'col', axis=1, tiled=True)]
    concatenate x0 -> x8, other arithmetic: none -> 42 us  [the longest x4 38.9 us: move_flows_on_mesh(): return jnp.roll(z2, val * found_now, 1)]
    reduce_scatter x2, waiting for transfers between devices: 53.1 us -> 15.8 us  [micro_step(): lax.psum_scatter(attn_out_grad, ('dp', 'row'), scatter_dimension=0, tiled...]
  transfers between devices with their start and end apart: 28 -> 32, of which waited for: 24 -> 28; matrix products, arithmetic and copies ran while one was open for 13% -> 14% of each run, Pallas kernels for 0% -> 0%
where the time goes in v1:
time: 2270 us
  waiting for transfers between devices  1460 us (64%)
  blocking collectives  264 us (12%)
  matrix products  250 us (11%)
  other arithmetic  177 us (8%)
  local copies, waits for them, and re-layouts  93.9 us (4%)
    reduce_scatter x4, waiting for transfers between devices, input_total(): lax.psum_scatter(partial_rows, 'col', scatter_dimension=1, tiled=True)  442 us
    ppermute x8, waiting for transfers between devices, move_flows_on_mesh(): ppermute(z2, shard_axis, perm=[(num, (num - met_up) % everything) for num...  317 us
    reduce_scatter x2, waiting for transfers between devices, micro_step(): lax.psum_scatter(contract_last(active_low, full_out), 'col', scatter_dime...  220 us
    reduce_scatter x2, waiting for transfers between devices, micro_step(): lax.psum_scatter(contract_last(attended, full_attn_out), 'col', scatter_d...  213 us
    all_gather x2, waiting for transfers between devices, micro_step(): lax.all_gather(normed.astype(jnp.bfloat16), 'col', axis=1, tiled=True)  130 us
    psum x8, blocking collectives, row_totals(): return lax.psum((jnp.sum(first, axis=1), jnp.sum(second, axis=1)), 'col')  117 us
    reduce_scatter x2, waiting for transfers between devices, micro_step(): lax.psum_scatter(qkv_grad, ('dp', 'row'), scatter_dimension=0, tiled=True)  91.5 us
    all_gather x2, blocking collectives, micro_step(): lax.all_gather(w_qkv, ('dp', 'row'), axis=0, tiled=True)  70.2 us
  transfers between devices with their start and end apart: 32, of which 28 were waited for; matrix products, arithmetic and copies ran while one was open for 14% of the time, Pallas kernels for 0%

profile of v1, /device:TPU:1, one launch (start us, length us, event | category | flops | bytes accessed | tf_op | source)
XLA Modules:
  0.0 2266.0 jit_solution(16612528704623265868)
XLA Ops:
  19.7 2205.3 %while.34 = (s32[]{:T(128)}, f32[96,3,192]{2,0,1:T(8,128)}, f32[96,192]{1,0:T(8,128)}, f32[96,768]{1,0:T(8,128)}, f32[96,768]{1,0:T(8,128)}, /*index=5*/f32[2,19...) while((s32[]{:T(128)}, f32[96,3,192]{2,0,1:T(8,128)}, ...), condition=%wide.region_41.43_spmd.clone.clone, body=%wide.region_0.42_spmd.clone.clone.sunk | while | flops 26897362944 | bytes 1096088704 | solution.py:290
  21.7 35.5 %all_gather.38 = bf16[768,3,192]{2,1,0:T(4,128)(2,1)S(1)} all-gather(bf16[96,3,192]{2,1,0:T(4,128)(2,1)} %get-tuple-element.924), channel_id=1, replica_groups=mesh['dp'=2,'row'=4,'col'=4] {'dp','row'}, dimensions={0}, use_global_device_ids=true | all-gather | bytes 995328 | tf_op jit(solution)/shard_map/while/body/eval_jaxpr/all_gather | solution.py:184
  59.5 24.1 %all_gather.39 = bf16[768,192]{1,0:T(8,128)(2,1)S(1)} all-gather(bf16[96,192]{1,0:T(8,128)(2,1)S(1)} %copy-done.52), channel_id=1, replica_groups=mesh['dp'=2,'row'=4,'col'=4] {'dp','row'}, dimensions={0}, use_global_device_ids=true | all-gather | bytes 331776 | tf_op jit(solution)/shard_map/while/body/eval_jaxpr/all_gather | solution.py:185
  131.1 106.2 %reduce-scatter.9.cloned.1.call-done = f32[2048,192]{0,1:T(8,128)} async-done(((f32[2048,768]{0,1:T(8,128)}), f32[2048,192]{0,1:T(8,128)}) %reduce-scatter.9.cloned.1.call-update) | async-done | bytes 1572880 | tf_op jit(solution)/shard_map/while/body/eval_jaxpr/reduce_scatter | solution.py:203
  264.1 64.9 %all-gather.11.cloned.1.call-done = bf16[2048,768]{0,1:T(8,128)(2,1)} async-done(((bf16[2048,192]{0,1:T(8,128)(2,1)}), bf16[2048,768]{0,1:T(8,128)(2,1)}) %all-gather.11.cloned.1.call-update) | async-done | bytes 3145744 | tf_op jit(solution)/shard_map/while/body/eval_jaxpr/all_gather | solution.py:208
  329.0 19.3 multiply_convert_fusion.7
  362.0 109.8 %reduce-scatter.11.cloned.1.call-done = f32[2048,192]{0,1:T(8,128)} async-done(((f32[2048,768]{0,1:T(8,128)}), f32[2048,192]{0,1:T(8,128)}) %reduce-scatter.11.cloned.1.call-update) | async-done | bytes 1572880 | tf_op jit(solution)/shard_map/while/body/eval_jaxpr/reduce_scatter | solution.py:211
  523.0 68.3 %collective-permute-done.1 = bf16[2048,384]{0,1:T(8,128)(2,1)} collective-permute-done((bf16[2048,384]{0,1:T(8,128)(2,1)}, bf16[2048,384]{0,1:T(8,128)(2,1)}, u32[]{:S(2)}, u32[]{:S(2)}) %collective-permute-start.1) | collective-permute-done | bytes 1572896 | tf_op jit(solution)/shard_map/while/body/eval_jaxpr/ppermute | solution.py:54
  622.9 109.9 %reduce-scatter.13.cloned.1.call-done = f32[2048,192]{0,1:T(8,128)} async-done(((f32[2048,768]{0,1:T(8,128)}), f32[2048,192]{0,1:T(8,128)}) %reduce-scatter.13.cloned.1.call-update) | async-done | bytes 1572880 | tf_op jit(solution)/shard_map/while/body/eval_jaxpr/reduce_scatter | solution.py:37
  777.5 64.7 %collective-permute-done.3 = bf16[2048,384]{0,1:T(8,128)(2,1)} collective-permute-done((bf16[2048,384]{0,1:T(8,128)(2,1)S(1)}, bf16[2048,384]{0,1:T(8,128)(2,1)}, u32[]{:S(2)}, u32[]{:S(2)}) %collective-permute-start.3) | collective-permute-done | bytes 1572896 | tf_op jit(solution)/shard_map/while/body/eval_jaxpr/ppermute | solution.py:54
  960.6 45.7 %reduce-scatter.15.cloned.1.call-done = f32[96,3,192]{2,0,1:T(8,128)} async-done(((f32[768,3,192]{2,0,1:T(8,128)}), f32[96,3,192]{2,0,1:T(8,128)}) %reduce-scatter.15.cloned.1.call-update) | async-done | bytes 221200 | tf_op jit(solution)/shard_map/while/body/eval_jaxpr/reduce_scatter | solution.py:265
  1008.0 111.3 %reduce-scatter.23.cloned.1.call-done = f32[2048,192]{0,1:T(8,128)} async-done(((f32[2048,768]{0,1:T(8,128)}), f32[2048,192]{0,1:T(8,128)}) %reduce-scatter.23.cloned.1.call-update) | async-done | bytes 1572880 | tf_op jit(solution)/shard_map/while/body/eval_jaxpr/reduce_scatter | solution.py:37
  1124.6 34.6 %all_gather.38 = bf16[768,3,192]{2,1,0:T(4,128)(2,1)S(1)} all-gather(bf16[96,3,192]{2,1,0:T(4,128)(2,1)} %get-tuple-element.924), channel_id=1, replica_groups=mesh['dp'=2,'row'=4,'col'=4] {'dp','row'}, dimensions={0}, use_global_device_ids=true | all-gather | bytes 995328 | tf_op jit(solution)/shard_map/while/body/eval_jaxpr/all_gather | solution.py:184
  1161.4 24.2 %all_gather.39 = bf16[768,192]{1,0:T(8,128)(2,1)S(1)} all-gather(bf16[96,192]{1,0:T(8,128)(2,1)S(1)} %copy-done.52), channel_id=1, replica_groups=mesh['dp'=2,'row'=4,'col'=4] {'dp','row'}, dimensions={0}, use_global_device_ids=true | all-gather | bytes 331776 | tf_op jit(solution)/shard_map/while/body/eval_jaxpr/all_gather | solution.py:185
  1231.9 106.4 %reduce-scatter.9.cloned.1.call-done = f32[2048,192]{0,1:T(8,128)} async-done(((f32[2048,768]{0,1:T(8,128)}), f32[2048,192]{0,1:T(8,128)}) %reduce-scatter.9.cloned.1.call-update) | async-done | bytes 1572880 | tf_op jit(solution)/shard_map/while/body/eval_jaxpr/reduce_scatter | solution.py:203
  1364.9 64.9 %all-gather.11.cloned.1.call-done = bf16[2048,768]{0,1:T(8,128)(2,1)} async-done(((bf16[2048,192]{0,1:T(8,128)(2,1)}), bf16[2048,768]{0,1:T(8,128)(2,1)}) %all-gather.11.cloned.1.call-update) | async-done | bytes 3145744 | tf_op jit(solution)/shard_map/while/body/eval_jaxpr/all_gather | solution.py:208
  1429.8 19.3 multiply_convert_fusion.7
  1462.8 109.8 %reduce-scatter.11.cloned.1.call-done = f32[2048,192]{0,1:T(8,128)} async-done(((f32[2048,768]{0,1:T(8,128)}), f32[2048,192]{0,1:T(8,128)}) %reduce-scatter.11.cloned.1.call-update) | async-done | bytes 1572880 | tf_op jit(solution)/shard_map/while/body/eval_jaxpr/reduce_scatter | solution.py:211
  1624.0 68.3 %collective-permute-done.1 = bf16[2048,384]{0,1:T(8,128)(2,1)} collective-permute-done((bf16[2048,384]{0,1:T(8,128)(2,1)}, bf16[2048,384]{0,1:T(8,128)(2,1)}, u32[]{:S(2)}, u32[]{:S(2)}) %collective-permute-start.1) | collective-permute-done | bytes 1572896 | tf_op jit(solution)/shard_map/while/body/eval_jaxpr/ppermute | solution.py:54
  1723.9 109.9 %reduce-scatter.13.cloned.1.call-done = f32[2048,192]{0,1:T(8,128)} async-done(((f32[2048,768]{0,1:T(8,128)}), f32[2048,192]{0,1:T(8,128)}) %reduce-scatter.13.cloned.1.call-update) | async-done | bytes 1572880 | tf_op jit(solution)/shard_map/while/body/eval_jaxpr/reduce_scatter | solution.py:37
  1878.2 64.7 %collective-permute-done.3 = bf16[2048,384]{0,1:T(8,128)(2,1)} collective-permute-done((bf16[2048,384]{0,1:T(8,128)(2,1)S(1)}, bf16[2048,384]{0,1:T(8,128)(2,1)}, u32[]{:S(2)}, u32[]{:S(2)}) %collective-permute-start.3) | collective-permute-done | bytes 1572896 | tf_op jit(solution)/shard_map/while/body/eval_jaxpr/ppermute | solution.py:54
  2061.9 45.7 %reduce-scatter.15.cloned.1.call-done = f32[96,3,192]{2,0,1:T(8,128)} async-done(((f32[768,3,192]{2,0,1:T(8,128)}), f32[96,3,192]{2,0,1:T(8,128)}) %reduce-scatter.15.cloned.1.call-update) | async-done | bytes 221200 | tf_op jit(solution)/shard_map/while/body/eval_jaxpr/reduce_scatter | solution.py:265
  2109.4 111.3 %reduce-scatter.23.cloned.1.call-done = f32[2048,192]{0,1:T(8,128)} async-done(((f32[2048,768]{0,1:T(8,128)}), f32[2048,192]{0,1:T(8,128)}) %reduce-scatter.23.cloned.1.call-update) | async-done | bytes 1572880 | tf_op jit(solution)/shard_map/while/body/eval_jaxpr/reduce_scatter | solution.py:37
  2229.2 27.9 %all-reduce.4 = (f32[2,192]{1,0:T(2,128)}, f32[192]{0:T(256)}, f32[768]{0:T(1024)}, f32[192]{0:T(256)}, f32[2,192]{1,0:T(2,128)}, /*index=5*/f32[2,192]{1,0:T(2,128)}) all-reduce(f32[2,192]{1,0:T(2,128)S(1)} %copy-done.61, f32[192]{0:T(256)S(1)} %copy-done.63, ...), channel_id=1, replica_groups=mesh['dp'=2,'row'=4,'col'=4] {'dp','row'}, use_global_device_ids=true, to_apply=%region_42.44 | all-reduce | flops 2304 | bytes 18432 | tf_op jit(solution)/shard_map/psum | solution.py:292
  (599 shorter events, 700.7 us)
Async XLA Ops:
  20.7 216.5 %reduce-scatter.9.cloned.1.call-start = ((), (), s32[]{:S(2)}) async-start(), calls=%async_computation.9 | async-start | bytes 7864320 | tf_op jit(solution)/shard_map/while/body/eval_jaxpr/reduce_scatter | solution.py:203
  127.6 136.5 %all-gather.13.cloned.1.call-start = ((), (), s32[]{:S(2)}) async-start(), calls=%async_computation.11 | async-start | bytes 1327104 | tf_op jit(solution)/shard_map/while/body/eval_jaxpr/all_gather | solution.py:186
  128.3 200.6 %all-gather.11.cloned.1.call-start = ((), (), s32[]{:S(2)}) async-start(), calls=%async_computation.10 | async-start | bytes 3932160 | tf_op jit(solution)/shard_map/while/body/eval_jaxpr/all_gather | solution.py:208
  255.5 98.3 %all-gather.15.cloned.1.call-start = ((), (), s32[]{:S(2)}) async-start(), calls=%async_computation.12 | async-start | bytes 1327104 | tf_op jit(solution)/shard_map/while/body/eval_jaxpr/all_gather | solution.py:187
  256.1 215.7 %reduce-scatter.11.cloned.1.call-start = ((), (), s32[]{:S(2)}) async-start(), calls=%async_computation.13 | async-start | bytes 7864320 | tf_op jit(solution)/shard_map/while/body/eval_jaxpr/reduce_scatter | solution.py:211
  361.3 371.5 %reduce-scatter.13.cloned.1.call-start = ((), (), s32[]{:S(2)}) async-start(), calls=%async_computation.14 | async-start | bytes 7864320 | tf_op jit(solution)/shard_map/while/body/eval_jaxpr/reduce_scatter | solution.py:37
  615.9 326.6 %reduce-scatter.19.cloned.1.call-start = ((), (), s32[]{:S(2)}) async-start(), calls=%async_computation.17 | async-start | bytes 2654208 | tf_op jit(solution)/shard_map/while/body/eval_jaxpr/reduce_scatter | solution.py:267
  622.9 321.4 %reduce-scatter.21.cloned.1.call-start = ((), (), s32[]{:S(2)}) async-start(), calls=%async_computation.18 | async-start | bytes 2654208 | tf_op jit(solution)/shard_map/while/body/eval_jaxpr/reduce_scatter | solution.py:268
  771.7 70.5 %collective-permute-start.3 = (bf16[2048,384]{0,1:T(8,128)(2,1)S(1)}, bf16[2048,384]{0,1:T(8,128)(2,1)}, u32[]{:S(2)}, u32[]{:S(2)}) collective-permute-start(bf16[2048,384]{0,1:T(8,128)(2,1)S(1)} %pad_maximum_fusion.10), channel_id=1, source_target_pairs={{0,2},{1,3},{2,0},{3,1},{4,6},{5,7},{6,4},{7,5},{8,10},{9,11},{10,... | collective-permute-start | bytes 4718600 | tf_op jit(solution)/shard_map/while/body/eval_jaxpr/ppermute | solution.py:54
  777.1 182.5 %reduce-scatter.17.cloned.1.call-start = ((), (), s32[]{:S(2)}) async-start(), calls=%async_computation.16 | async-start | bytes 884736 | tf_op jit(solution)/shard_map/while/body/eval_jaxpr/reduce_scatter | solution.py:266
  924.1 82.2 %reduce-scatter.15.cloned.1.call-start = ((), (), s32[]{:S(2)}) async-start(), calls=%async_computation.15 | async-start | bytes 2654208 | tf_op jit(solution)/shard_map/while/body/eval_jaxpr/reduce_scatter | solution.py:265
  932.8 186.5 %reduce-scatter.23.cloned.1.call-start = ((), (), s32[]{:S(2)}) async-start(), calls=%async_computation.19 | async-start | bytes 7864320 | tf_op jit(solution)/shard_map/while/body/eval_jaxpr/reduce_scatter | solution.py:37
  1123.6 214.7 %reduce-scatter.9.cloned.1.call-start = ((), (), s32[]{:S(2)}) async-start(), calls=%async_computation.9 | async-start | bytes 7864320 | tf_op jit(solution)/shard_map/while/body/eval_jaxpr/reduce_scatter | solution.py:203
  1228.6 136.3 %all-gather.13.cloned.1.call-start = ((), (), s32[]{:S(2)}) async-start(), calls=%async_computation.11 | async-start | bytes 1327104 | tf_op jit(solution)/shard_map/while/body/eval_jaxpr/all_gather | solution.py:186
  1229.2 200.6 %all-gather.11.cloned.1.call-start = ((), (), s32[]{:S(2)}) async-start(), calls=%async_computation.10 | async-start | bytes 3932160 | tf_op jit(solution)/shard_map/while/body/eval_jaxpr/all_gather | solution.py:208
  1356.5 98.2 %all-gather.15.cloned.1.call-start = ((), (), s32[]{:S(2)}) async-start(), calls=%async_computation.12 | async-start | bytes 1327104 | tf_op jit(solution)/shard_map/while/body/eval_jaxpr/all_gather | solution.py:187
  1357.1 215.6 %reduce-scatter.11.cloned.1.call-start = ((), (), s32[]{:S(2)}) async-start(), calls=%async_computation.13 | async-start | bytes 7864320 | tf_op jit(solution)/shard_map/while/body/eval_jaxpr/reduce_scatter | solution.py:211
  1462.2 371.7 %reduce-scatter.13.cloned.1.call-start = ((), (), s32[]{:S(2)}) async-start(), calls=%async_computation.14 | async-start | bytes 7864320 | tf_op jit(solution)/shard_map/while/body/eval_jaxpr/reduce_scatter | solution.py:37
  1716.9 326.6 %reduce-scatter.19.cloned.1.call-start = ((), (), s32[]{:S(2)}) async-start(), calls=%async_computation.17 | async-start | bytes 2654208 | tf_op jit(solution)/shard_map/while/body/eval_jaxpr/reduce_scatter | solution.py:267
  1723.9 321.4 %reduce-scatter.21.cloned.1.call-start = ((), (), s32[]{:S(2)}) async-start(), calls=%async_computation.18 | async-start | bytes 2654208 | tf_op jit(solution)/shard_map/while/body/eval_jaxpr/reduce_scatter | solution.py:268
  1872.6 70.4 %collective-permute-start.3 = (bf16[2048,384]{0,1:T(8,128)(2,1)S(1)}, bf16[2048,384]{0,1:T(8,128)(2,1)}, u32[]{:S(2)}, u32[]{:S(2)}) collective-permute-start(bf16[2048,384]{0,1:T(8,128)(2,1)S(1)} %pad_maximum_fusion.10), channel_id=1, source_target_pairs={{0,2},{1,3},{2,0},{3,1},{4,6},{5,7},{6,4},{7,5},{8,10},{9,11},{10,... | collective-permute-start | bytes 4718600 | tf_op jit(solution)/shard_map/while/body/eval_jaxpr/ppermute | solution.py:54
  1878.0 182.9 %reduce-scatter.17.cloned.1.call-start = ((), (), s32[]{:S(2)}) async-start(), calls=%async_computation.16 | async-start | bytes 884736 | tf_op jit(solution)/shard_map/while/body/eval_jaxpr/reduce_scatter | solution.py:266
  2025.1 82.5 %reduce-scatter.15.cloned.1.call-start = ((), (), s32[]{:S(2)}) async-start(), calls=%async_computation.15 | async-start | bytes 2654208 | tf_op jit(solution)/shard_map/while/body/eval_jaxpr/reduce_scatter | solution.py:265
  2033.8 186.9 %reduce-scatter.23.cloned.1.call-start = ((), (), s32[]{:S(2)}) async-start(), calls=%async_computation.19 | async-start | bytes 7864320 | tf_op jit(solution)/shard_map/while/body/eval_jaxpr/reduce_scatter | solution.py:37
  (157 other events, 4610.6 us)
Sparse Core Ops, SparseCore 0:
  22.6 65.3 all-gather.8
  127.7 109.5 reduce-scatter.8
  239.2 24.8 all-gather.12
  266.1 62.8 all-gather.10
  330.7 23.1 all-gather.14
  361.5 110.3 reduce-scatter.10
  616.0 116.7 reduce-scatter.12
  736.2 42.7 reduce-scatter.18
  782.3 43.9 reduce-scatter.20
  924.2 35.3 reduce-scatter.16
  963.6 42.7 reduce-scatter.14
  1008.5 110.8 reduce-scatter.22
  1125.5 63.8 all-gather.8
  1228.7 109.5 reduce-scatter.8
  1340.0 24.8 all-gather.12
  1366.9 62.8 all-gather.10
  1431.5 23.1 all-gather.14
  1462.3 110.3 reduce-scatter.10
  1717.0 116.7 reduce-scatter.12
  1837.1 42.7 reduce-scatter.18
  1883.2 44.0 reduce-scatter.20
  2025.2 35.6 reduce-scatter.16
  2064.9 42.6 reduce-scatter.14
  2109.7 110.8 reduce-scatter.22
